TPU v7x, 256 devices: a whole 4x4x8 slice. The times are simulated.
256 devices in a mesh: row: 16 (over x, y_hi, core), col: 16 (over y_lo, z).
Axes of the slice: x: 4, y: 4 (y_hi: 2, y_lo: 2; y = y_hi * 2 + y_lo), z: 8, core: 2. Of those that a mesh axis runs over, the one named last changes fastest.
Arguments:
- query_in: bfloat16 [4096, 8192], P('row', 'col'), may hold values from -6 to 6
- key_in: bfloat16 [4096, 8192], P('row', 'col'), may hold values from -6 to 6
- value_in: bfloat16 [4096, 8192], P('row', 'col'), may hold values from -6 to 6
- filters: float32 [512, 128], P('col'), may hold values from -0.5 to 0.5
- out_weight: bfloat16 [8192, 8192], P('row', 'col'), may hold values from -0.0625 to 0.0625
- out_grad: bfloat16 [4096, 8192], P('row', 'col'), may hold values from -6 to 6
Outputs:
- mixed: bfloat16 [4096, 8192], P('row', 'col')
- query_grad: bfloat16 [4096, 8192], P('row', 'col')
- key_grad: bfloat16 [4096, 8192], P('row', 'col')
- value_grad: bfloat16 [4096, 8192], P('row', 'col')
- weight_grad: bfloat16 [8192, 8192], P('row', 'col')
- filter_grad: float32 [512, 128], P('col')
All inputs are finite; a program needn't handle non-finite values.
Results may differ from a plain program's by a relative error of at most 0.018.
Values may be sent and summed in bfloat16 or wider, within the bound.
A program may use at most 128 MiB of HBM per device.

v0:
```python
import math
import jax
import jax.numpy as jnp
from jax import lax
from jax.sharding import PartitionSpec as P


def from_behind(shard, axis, by):
    size = lax.axis_size(axis)
    pairs = [(i, i + by) for i in range(size) if 0 <= i + by < size]
    return lax.ppermute(shard, axis, pairs)


def toeplitz(taps, causal):
    groups, span = taps.shape
    if causal:
        template = jnp.concatenate(
            [
                jnp.zeros((groups, 1), jnp.float32),
                taps[:, ::-1],
                jnp.zeros((groups, span), jnp.float32),
            ],
            1,
        )
    else:
        template = jnp.concatenate([taps, jnp.zeros((groups, span + 1), jnp.float32)], 1)
    tiled = jnp.tile(template, (1, span))
    return tiled[:, : 2 * span * span].reshape(groups, span, 2 * span)


def windows(extended, span):
    count = (extended.shape[0] - span) // span
    first = extended[:-span].reshape(count, span, extended.shape[1])
    second = extended[span:].reshape(count, span, extended.shape[1])
    return jnp.concatenate([first, second], axis=1)


def convolve(matrix, extended, span, group):
    blocks = windows(extended, span)
    count, _, width = blocks.shape
    split = blocks.reshape(count, 2 * span, width // group, group)
    result = jnp.einsum("gts,bsgc->btgc", matrix, split, precision=lax.Precision.HIGHEST)
    return result.reshape(count * span, width)


def shards(query_in, key_in, value_in, filters, out_weight, out_grad):
    f32 = jnp.float32
    bf16 = jnp.bfloat16
    tokens, width = query_in.shape
    span = filters.shape[1]
    group = width // filters.shape[0]
    total_tokens = tokens * lax.axis_size("row")
    key32 = key_in.astype(f32)
    value32 = value_in.astype(f32)
    query32 = query_in.astype(f32)
    product = key32 * value32
    key_rim, value_rim = from_behind((key_in[-span:], value_in[-span:]), "row", 1)
    product_rim = key_rim.astype(f32) * value_rim.astype(f32)
    product_ext = jnp.concatenate([product_rim, product], 0)
    conv = convolve(toeplitz(filters, True), product_ext, span, group)
    gated = (query32 * conv).astype(bf16)
    panel = lax.all_gather(gated, "col", axis=1, tiled=True)
    weights = lax.all_gather(out_weight, "row", axis=0, tiled=True)
    mixed_sum = jnp.dot(panel, weights, preferred_element_type=f32)
    partial_value = lax.dot_general(
        out_grad, weights, (((1,), (1,)), ((), ())), preferred_element_type=f32
    )
    mixed = mixed_sum.astype(bf16)
    grad_gated = lax.psum_scatter(
        partial_value.astype(jnp.bfloat16), "col", scatter_dimension=1, tiled=True
    ).astype(jnp.float32)
    query_grad = (grad_gated * conv).astype(bf16)
    grad_conv = grad_gated * query32
    grad_rim = from_behind(grad_conv[:span].astype(jnp.bfloat16), "row", -1).astype(jnp.float32)
    grad_ext = jnp.concatenate([grad_conv, grad_rim], 0)
    grad_product = convolve(toeplitz(filters, False), grad_ext, span, group)
    key_grad = (grad_product * value32).astype(bf16)
    value_grad = (grad_product * key32).astype(bf16)
    count = tokens // span
    groups = width // group
    grad_blocks = grad_conv.reshape(count, span, groups, group)
    product_blocks = windows(product_ext, span).reshape(count, 2 * span, groups, group)
    corr = jnp.einsum(
        "btgc,bsgc->gts", grad_blocks, product_blocks, precision=lax.Precision.HIGHEST
    )
    flat = jnp.concatenate(
        [corr.reshape(groups, 2 * span * span), jnp.zeros((groups, span), f32)], 1
    )
    skewed = flat.reshape(groups, span, 2 * span + 1)[:, :, 1 : span + 1]
    local_taps = jnp.sum(skewed, axis=1)[:, ::-1]
    filter_grad = lax.psum(local_taps, "row") * (1.0 / math.sqrt(total_tokens * group))
    weight_sum = lax.psum_scatter(
        lax.dot_general(
            panel, out_grad, (((0,), (0,)), ((), ())), preferred_element_type=f32
        ).astype(jnp.bfloat16),
        "row",
        scatter_dimension=0,
        tiled=True,
    ).astype(jnp.float32)
    weight_grad = (weight_sum * (1.0 / math.sqrt(total_tokens))).astype(bf16)
    return (mixed, query_grad, key_grad, value_grad, weight_grad, filter_grad)


def solution(mesh):
    placed = (
        P("row", "col"),
        P("row", "col"),
        P("row", "col"),
        P("col", None),
        P("row", "col"),
        P("row", "col"),
    )
    return jax.shard_map(
        shards,
        mesh=mesh,
        in_specs=placed,
        out_specs=(
            P("row", "col"),
            P("row", "col"),
            P("row", "col"),
            P("row", "col"),
            P("row", "col"),
            P("col", None),
        ),
        check_vma=False,
    )
```

profile of v0, /device:TPU:2, one launch (start us, length us, event | category | flops | bytes accessed | tf_op | source)
XLA Modules:
  0.0 399.6 jit_solution(14120310710008545654)
XLA Ops:
  7.2 0.7 all-gather.5.cloned.1.call-update
  8.0 82.3 %all-gather.5.cloned.1.call-done = bf16[8192,512]{1,0:T(8,128)(2,1)} async-done(((bf16[512,512]{1,0:T(8,128)(2,1)}), bf16[8192,512]{1,0:T(8,128)(2,1)}) %all-gather.5.cloned.1.call-update) | async-done | bytes 8388624 | tf_op jit(solution)/shard_map/all_gather | solution.py:63
  90.2 7.8 %convolution_convert_fusion.1 = bf16[256,8192]{1,0:T(8,128)(2,1)} fusion(bf16[256,512]{1,0:T(8,128)(2,1)S(1)} %copy-done, bf16[8192,512]{1,0:T(8,128)(2,1)} %all-gather.5.cloned.1.call-done), kind=kOutput, calls=%fused_computation.1 | convolution fusion | flops 2149580800 | bytes 12845056 | tf_op jit(solution)/shard_map/dot_general | solution.py:65
  98.1 0.9 copy-done.6
  99.2 2.1 collective-permute-start
  101.3 0.1 copy.16
  101.5 2.3 collective-permute-start.1
  103.9 3.1 tile.20
  107.0 6.7 %tile.21 = f32[32,32896]{1,0:T(8,128)} reshape(f32[32,128,257]{2,1,0:T(8,128)} %tile.20) | data formatting | bytes 8421376 | tf_op jit(solution)/shard_map/tile | solution.py:27
  113.7 2.2 slice-done
  115.9 3.3 copy.37
  119.4 3.1 tile.8
  122.5 6.7 %tile.9 = f32[32,32896]{1,0:T(8,128)} reshape(f32[32,128,257]{2,1,0:T(8,128)} %tile.8) | data formatting | bytes 8421376 | tf_op jit(solution)/shard_map/tile | solution.py:27
  129.2 2.2 slice-done.1
  131.4 3.2 copy.35
  134.6 44.5 %reduce-scatter.3.cloned.1.call-done = bf16[256,512]{1,0:T(8,128)(2,1)} async-done(((bf16[256,8192]{1,0:T(8,128)(2,1)}), bf16[256,512]{1,0:T(8,128)(2,1)}) %reduce-scatter.3.cloned.1.call-update) | async-done | bytes 262160 | tf_op jit(solution)/shard_map/reduce_scatter | solution.py:69
  179.1 1.0 convert_multiply_fusion
  180.2 0.7 slice.42
  180.8 2.1 collective-permute-start.2
  183.0 0.2 copy.24
  183.2 0.3 concatenate.37
  183.5 2.0 collective-permute-done.2
  185.6 0.2 copy.25
  185.8 0.3 concatenate.39
  186.2 5.9 %fusion.7 = f32[2,128,32,16]{1,3,0,2:T(8,128)S(1)} fusion(f32[32,128,256,1]{2,1,0,3:T(8,128)} %bitcast.60, f32[2,128,32,16]{1,3,0,2:T(8,128)S(1)} %copy.27, f32[2,128,32,16]{1,3,0,2:T(8,128)S(1)} %copy.26), kind=kOutput, calls=%fused_computation.8 | convolution fusion | flops 402915328 | bytes 5767168 | tf_op jit(solution)/shard_map/gts,bsgc->btgc/dot_general | solution.py:42
  192.1 0.3 copy.28
  192.4 0.9 fusion.14
  193.3 0.3 concatenate.34
  193.6 0.3 concatenate.33
  194.0 5.9 %fusion.4 = f32[2,128,32,16]{1,3,0,2:T(8,128)S(1)} fusion(f32[2,256,32,16]{1,3,0,2:T(8,128)S(1)} %copy_dynamic-update-slice_fusion, f32[32,128,256,1]{2,1,0,3:T(8,128)} %bitcast.59), kind=kOutput, calls=%fused_computation.7 | convolution fusion | flops 402653184 | bytes 5767168 | tf_op jit(solution)/shard_map/gts,bsgc->btgc/dot_general | solution.py:42
  200.0 0.3 copy.21
  200.3 0.2 copy.22
  200.5 0.9 fusion.16
  201.4 0.3 reduce-scatter.5.cloned.1.call-start
  201.7 73.7 %all-gather.3.cloned.1.call-done = bf16[256,8192]{1,0:T(8,128)(2,1)} async-done(((bf16[256,512]{1,0:T(8,128)(2,1)}), bf16[256,8192]{1,0:T(8,128)(2,1)}) %all-gather.3.cloned.1.call-update) | async-done | bytes 4194320 | tf_op jit(solution)/shard_map/all_gather | solution.py:62
  275.4 7.8 %convolution_convert_fusion = bf16[8192,512]{1,0:T(8,128)(2,1)} fusion(bf16[256,8192]{1,0:T(8,128)(2,1)} %all-gather.3.cloned.1.call-done, bf16[256,512]{1,0:T(8,128)(2,1)S(1)} %copy-done), kind=kOutput, calls=%fused_computation | convolution fusion | flops 2151677952 | bytes 12845056 | tf_op jit(solution)/shard_map/dot_general | solution.py:93
  283.2 3.5 fusion.18
  286.7 2.4 copy.39
  289.2 2.3 concatenate.42
  291.5 8.2 %reshape.61 = f32[32,128,257]{2,1,0:T(8,128)} reshape(f32[32,32896]{1,0:T(8,128)} %concatenate.42) | data formatting | bytes 8421376 | tf_op jit(solution)/shard_map/reshape | solution.py:89
  299.7 3.2 slice_reduce_fusion
  303.0 0.8 copy.30
  303.9 0.8 copy.31
  304.7 57.5 %psum.7 = f32[32,128]{1,0:T(8,128)S(1)} all-reduce(f32[32,128]{1,0:T(8,128)S(1)} %rev.7), channel_id=1, replica_groups=mesh['row'=16,'col'=16] {'row'}, use_global_device_ids=true, to_apply=%region_3.0 | all-reduce | flops 4096 | bytes 32768 | tf_op jit(solution)/shard_map/psum | solution.py:91
  362.3 0.6 broadcast_multiply_fusion
  362.9 7.7 %convolution_convert_fusion.2 = bf16[256,512]{1,0:T(8,128)(2,1)} fusion(bf16[256,8192]{1,0:T(8,128)(2,1)} %all-gather.3.cloned.1.call-done, bf16[8192,512]{1,0:T(8,128)(2,1)} %all-gather.5.cloned.1.call-done), kind=kOutput, calls=%fused_computation.9 | convolution fusion | flops 2147614720 | bytes 12845056 | tf_op jit(solution)/shard_map/dot_general | solution.py:64
  370.6 20.6 %reduce-scatter.5.cloned.1.call-done = bf16[512,512]{1,0:T(8,128)(2,1)} async-done(((bf16[8192,512]{1,0:T(8,128)(2,1)}), bf16[512,512]{1,0:T(8,128)(2,1)}) %reduce-scatter.5.cloned.1.call-update) | async-done | bytes 524304 | tf_op jit(solution)/shard_map/reduce_scatter | solution.py:92
  391.2 1.9 multiply_convert_fusion
  (46 shorter events, 1.0 us)
Async XLA Ops:
  7.2 83.1 %copy-start = (bf16[256,512]{1,0:T(8,128)(2,1)S(1)}, bf16[256,512]{1,0:T(8,128)(2,1)}, u32[]{:S(2)}) copy-start(bf16[256,512]{1,0:T(8,128)(2,1)} %param.11) | copy-start | bytes 786436
  7.2 83.1 %all-gather.5.cloned.1.call-start = ((), (), s32[]{:S(2)}) async-start(), calls=%async_computation.3 | async-start | bytes 8912896 | tf_op jit(solution)/shard_map/all_gather | solution.py:63
  7.9 171.2 %reduce-scatter.3.cloned.1.call-start = ((), (), s32[]{:S(2)}) async-start(), calls=%async_computation.4 | async-start | bytes 4456448 | tf_op jit(solution)/shard_map/reduce_scatter | solution.py:69
  98.0 0.9 copy-start.6
  98.1 3.2 copy-start.7
  98.1 5.7 %copy-start.8 = (f32[32,128]{1,0:T(8,128)S(1)}, f32[32,128]{1,0:T(8,128)}, u32[]{:S(2)}) copy-start(f32[32,128]{1,0:T(8,128)} %param.9) | copy-start | bytes 49156
  98.1 177.3 %all-gather.3.cloned.1.call-start = ((), (), s32[]{:S(2)}) async-start(), calls=%async_computation.2 | async-start | bytes 4456448 | tf_op jit(solution)/shard_map/all_gather | solution.py:62
  99.2 83.8 %collective-permute-start = (bf16[128,512]{0,1:T(8,128)(2,1)S(1)}, bf16[128,512]{0,1:T(8,128)(2,1)S(1)}, u32[]{:S(2)}, u32[]{:S(2)}) collective-permute-start(bf16[128,512]{0,1:T(8,128)(2,1)S(1)} %slice.34), channel_id=1, source_target_pairs={{0,16},{16,32},{32,48},{48,64},{64,80},{80,96},{96,112},{112,128},... | collective-permute-start | bytes 393224 | tf_op jit(solution)/shard_map/ppermute | solution.py:11
  101.5 81.5 %collective-permute-start.1 = (bf16[128,512]{0,1:T(8,128)(2,1)S(1)}, bf16[128,512]{0,1:T(8,128)(2,1)S(1)}, u32[]{:S(2)}, u32[]{:S(2)}) collective-permute-start(bf16[128,512]{0,1:T(8,128)(2,1)S(1)} %slice.35), channel_id=1, source_target_pairs={{0,16},{16,32},{32,48},{48,64},{64,80},{80,96},{96,112},{112,128},... | collective-permute-start | bytes 393224 | tf_op jit(solution)/shard_map/ppermute | solution.py:11
  113.7 2.2 slice-start
  129.2 2.2 slice-start.1
  131.4 47.7 %copy-start.2 = (bf16[256,512]{1,0:T(8,128)(2,1)S(1)}, bf16[256,512]{1,0:T(8,128)(2,1)}, u32[]{:S(2)}) copy-start(bf16[256,512]{1,0:T(8,128)(2,1)} %param.6) | copy-start | bytes 786436
  180.8 4.7 %collective-permute-start.2 = (bf16[128,512]{1,0:T(8,128)(2,1)}, bf16[128,512]{1,0:T(8,128)(2,1)S(1)}, u32[]{:S(2)}, u32[]{:S(2)}) collective-permute-start(bf16[128,512]{1,0:T(8,128)(2,1)} %slice.42), channel_id=1, source_target_pairs={{16,0},{32,16},{48,32},{64,48},{80,64},{96,80},{112,96},{128,112},... | collective-permute-start | bytes 393224 | tf_op jit(solution)/shard_map/ppermute | solution.py:11
  194.0 6.5 %copy-start.3 = (bf16[256,512]{1,0:T(8,128)(2,1)S(1)}, bf16[256,512]{1,0:T(8,128)(2,1)}, u32[]{:S(2)}) copy-start(bf16[256,512]{1,0:T(8,128)(2,1)} %reduce-scatter.3.cloned.1.call-done) | copy-start | bytes 786436
  201.4 189.7 %reduce-scatter.5.cloned.1.call-start = ((), (), s32[]{:S(2)}) async-start(), calls=%async_computation.5 | async-start | bytes 8912896 | tf_op jit(solution)/shard_map/reduce_scatter | solution.py:92
  291.5 11.5 %copy-start.5 = (bf16[256,512]{0,1:T(8,128)(2,1)S(1)}, bf16[256,512]{0,1:T(8,128)(2,1)}, u32[]{:S(2)}) copy-start(bf16[256,512]{0,1:T(8,128)(2,1)} %get-tuple-element.13) | copy-start | bytes 786436
  291.5 12.4 %copy-start.4 = (bf16[256,512]{0,1:T(8,128)(2,1)S(1)}, bf16[256,512]{0,1:T(8,128)(2,1)}, u32[]{:S(2)}) copy-start(bf16[256,512]{0,1:T(8,128)(2,1)} %get-tuple-element.12) | copy-start | bytes 786436
  362.9 30.2 %copy-start.1 = (bf16[256,512]{1,0:T(8,128)(2,1)S(1)}, bf16[256,512]{1,0:T(8,128)(2,1)}, u32[]{:S(2)}) copy-start(bf16[256,512]{1,0:T(8,128)(2,1)} %param.11) | copy-start | bytes 786436
Sparse Core Ops, SparseCore 0:
  10.7 79.5 all-gather.4
  98.2 80.8 reduce-scatter.2
  201.6 73.8 all-gather.2
  283.4 107.7 reduce-scatter.4
where the time goes:
time: 400 us
  waiting for transfers between devices  224 us (56%)
  blocking collectives  57.5 us (14%)
  local copies, waits for them, and re-layouts  49.8 us (12%)
  matrix products  38.7 us (10%)
  between operations  14.1 us (4%)
  other arithmetic  8.78 us (2%)
  starting transfers between devices  6.92 us (2%)
    all_gather x1, waiting for transfers between devices, shards(): weights = lax.all_gather(out_weight, 'row', axis=0, tiled=True)  82.3 us
    all_gather x1, waiting for transfers between devices, shards(): panel = lax.all_gather(gated, 'col', axis=1, tiled=True)  73.7 us
    psum x1, blocking collectives, shards(): lax.psum(local_taps, 'row') * (1.0 / math.sqrt(total_tokens * group))  57.5 us
    reduce_scatter x1, waiting for transfers between devices, shards(): lax.psum_scatter(partial_value.astype(jnp.bfloat16), 'col', scatter_dimen...  44.5 us
    reduce_scatter x1, waiting for transfers between devices, shards(): lax.psum_scatter(lax.dot_general(panel, out_grad, (((0,), (0,)), ((), ())...  20.6 us
    another operation x4, local copies, waits for them, and re-layouts, toeplitz(): tiled = jnp.tile(template, (1, span))  19.6 us
    unnamed x27, local copies, waits for them, and re-layouts  12 us
    dot_general x2, matrix products, convolve(): jnp.einsum('gts,bsgc->btgc', matrix, split, precision=lax.Precision.HIGHEST)  11.9 us
  transfers between devices with their start and end apart: 7, of which 5 were waited for; matrix products, arithmetic and copies ran while one was open for 15% of the time, Pallas kernels for 0%

commit v1 on v0

--- a/solution.py
+++ b/solution.py
@@ -59,7 +59,15 @@
     product_ext = jnp.concatenate([product_rim, product], 0)
     conv = convolve(toeplitz(filters, True), product_ext, span, group)
     gated = (query32 * conv).astype(bf16)
-    panel = lax.all_gather(gated, "col", axis=1, tiled=True)
+    panel = jnp.concatenate(
+        jax.lax.all_to_all(
+            jnp.stack([gated for _ in range(jax.lax.axis_size("col"))]),
+            split_axis=0,
+            axis_name="col",
+            concat_axis=0,
+        ),
+        axis=1,
+    )
     weights = lax.all_gather(out_weight, "row", axis=0, tiled=True)
     mixed_sum = jnp.dot(panel, weights, preferred_element_type=f32)
     partial_value = lax.dot_general(

time: 400 us -> 425 us (1.062)
  blocking collectives: 57.5 us -> 157 us
  waiting for transfers between devices: 224 us -> 149 us
    all_to_all x0 -> x1, blocking collectives: none -> 95.5 us  [shards(): jax.lax.all_to_all(jnp.stack([gated for _ in range(jax.lax.axis_size('col...]
    all_gather x1 -> x0, waiting for transfers between devices: 73.7 us -> none  [shards(): panel = lax.all_gather(gated, 'col', axis=1, tiled=True)]
  transfers between devices with their start and end apart: 7 -> 6, of which waited for: 5 -> 4; matrix products, arithmetic and copies ran while one was open for 15% -> 14% of each run, Pallas kernels for 0% -> 0%
where the time goes in v1:
time: 425 us; the launch traced here: 424 us
  blocking collectives  157 us (37%)
  waiting for transfers between devices  149 us (35%)
  local copies, waits for them, and re-layouts  52.2 us (12%)
  matrix products  36.4 us (9%)
  between operations  14.1 us (3%)
  other arithmetic  8.69 us (2%)
  starting transfers between devices  6.66 us (2%)
    all_to_all x1, blocking collectives, shards(): jax.lax.all_to_all(jnp.stack([gated for _ in range(jax.lax.axis_size('col...  95.5 us
    all_gather x1, waiting for transfers between devices, shards(): weights = lax.all_gather(out_weight, 'row', axis=0, tiled=True)  82.3 us
    psum x1, blocking collectives, shards(): lax.psum(local_taps, 'row') * (1.0 / math.sqrt(total_tokens * group))  61.5 us
    reduce_scatter x1, waiting for transfers between devices, shards(): lax.psum_scatter(partial_value.astype(jnp.bfloat16), 'col', scatter_dimen...  44.3 us
    reduce_scatter x1, waiting for transfers between devices, shards(): lax.psum_scatter(lax.dot_general(panel, out_grad, (((0,), (0,)), ((), ())...  19.7 us
    another operation x4, local copies, waits for them, and re-layouts, toeplitz(): tiled = jnp.tile(template, (1, span))  19.6 us
    unnamed x27, local copies, waits for them, and re-layouts  14 us
    dot_general x2, matrix products, convolve(): jnp.einsum('gts,bsgc->btgc', matrix, split, precision=lax.Precision.HIGHEST)  11.9 us
  transfers between devices with their start and end apart: 6, of which 4 were waited for; matrix products, arithmetic and copies ran while one was open for 14% of the time, Pallas kernels for 0%

profile of v1, /device:TPU:2, one launch (start us, length us, event | category | flops | bytes accessed | tf_op | source)
XLA Modules:
  0.0 424.2 jit_solution(544346793753258520)
XLA Ops:
  7.2 0.7 all-gather.2.cloned.1.call-update
  8.0 82.3 %all-gather.2.cloned.1.call-done = bf16[8192,512]{1,0:T(8,128)(2,1)} async-done(((bf16[512,512]{1,0:T(8,128)(2,1)}), bf16[8192,512]{1,0:T(8,128)(2,1)}) %all-gather.2.cloned.1.call-update) | async-done | bytes 8388624 | tf_op jit(solution)/shard_map/all_gather | solution.py:71
  90.2 7.8 %convolution_convert_fusion.1 = bf16[256,8192]{1,0:T(8,128)(2,1)} fusion(bf16[256,512]{1,0:T(8,128)(2,1)S(1)} %copy-done, bf16[8192,512]{1,0:T(8,128)(2,1)} %all-gather.2.cloned.1.call-done), kind=kOutput, calls=%fused_computation.1 | convolution fusion | flops 2149580800 | bytes 12845056 | tf_op jit(solution)/shard_map/dot_general | solution.py:73
  98.1 0.9 copy-done.6
  99.1 2.1 collective-permute-start
  101.5 2.3 collective-permute-start.1
  103.9 3.1 tile.20
  107.0 6.7 %tile.21 = f32[32,32896]{1,0:T(8,128)} reshape(f32[32,128,257]{2,1,0:T(8,128)} %tile.20) | data formatting | bytes 8421376 | tf_op jit(solution)/shard_map/tile | solution.py:27
  113.6 2.2 slice-done
  115.8 3.3 copy.38
  119.3 3.1 tile.8
  122.4 6.7 %tile.9 = f32[32,32896]{1,0:T(8,128)} reshape(f32[32,128,257]{2,1,0:T(8,128)} %tile.8) | data formatting | bytes 8421376 | tf_op jit(solution)/shard_map/tile | solution.py:27
  129.1 2.2 slice-done.1
  131.3 3.2 copy.36
  134.6 44.3 %reduce-scatter.3.cloned.1.call-done = bf16[256,512]{1,0:T(8,128)(2,1)} async-done(((bf16[256,8192]{1,0:T(8,128)(2,1)}), bf16[256,512]{1,0:T(8,128)(2,1)}) %reduce-scatter.3.cloned.1.call-update) | async-done | bytes 262160 | tf_op jit(solution)/shard_map/reduce_scatter | solution.py:77
  178.8 1.0 convert_multiply_fusion
  179.9 0.7 slice.42
  180.5 2.1 collective-permute-start.2
  182.7 0.2 copy.25
  182.9 0.3 concatenate.37
  183.2 2.0 collective-permute-done.2
  185.3 0.2 copy.26
  185.5 0.3 concatenate.39
  185.9 5.9 %fusion.7 = f32[2,128,32,16]{1,3,0,2:T(8,128)S(1)} fusion(f32[32,128,256,1]{2,1,0,3:T(8,128)} %bitcast.65, f32[2,128,32,16]{1,3,0,2:T(8,128)S(1)} %copy.28, f32[2,128,32,16]{1,3,0,2:T(8,128)S(1)} %copy.27), kind=kOutput, calls=%fused_computation.8 | convolution fusion | flops 402915328 | bytes 5767168 | tf_op jit(solution)/shard_map/gts,bsgc->btgc/dot_general | solution.py:42
  191.8 0.3 copy.29
  192.1 0.9 fusion.14
  193.0 0.3 concatenate.34
  193.3 0.3 concatenate.33
  193.7 5.9 %fusion.4 = f32[2,128,32,16]{1,3,0,2:T(8,128)S(1)} fusion(f32[2,256,32,16]{1,3,0,2:T(8,128)S(1)} %copy_dynamic-update-slice_fusion, f32[32,128,256,1]{2,1,0,3:T(8,128)} %bitcast.64), kind=kOutput, calls=%fused_computation.7 | convolution fusion | flops 402653184 | bytes 5767168 | tf_op jit(solution)/shard_map/gts,bsgc->btgc/dot_general | solution.py:42
  199.7 0.3 copy.21
  200.0 0.2 copy.22
  200.2 0.8 fusion.16
  201.2 0.4 stack.2
  201.6 95.5 %all_to_all.5 = bf16[16,256,512]{1,2,0:T(8,128)(2,1)S(1)} all-to-all(bf16[16,256,512]{1,2,0:T(8,128)(2,1)S(1)} %stack.2), channel_id=1, replica_groups=mesh['row'=16,'col'=16] {'col'}, dimensions={0} | all-to-all | bytes 8388608 | tf_op jit(solution)/shard_map/all_to_all | solution.py:63
  297.1 2.1 copy-done.1
  299.1 5.6 %convolution_convert_fusion = bf16[8192,512]{1,0:T(8,128)(2,1)} fusion(bf16[256,8192]{0,1:T(8,128)(2,1)S(1)} %bitcast.60, bf16[256,512]{1,0:T(8,128)(2,1)S(1)} %copy-done), kind=kOutput, calls=%fused_computation | convolution fusion | flops 2151677952 | bytes 12845056 | tf_op jit(solution)/shard_map/dot_general | solution.py:101
  304.8 3.5 fusion.18
  308.3 2.4 copy.40
  310.7 2.3 concatenate.42
  313.0 8.2 %reshape.71 = f32[32,128,257]{2,1,0:T(8,128)} reshape(f32[32,32896]{1,0:T(8,128)} %concatenate.42) | data formatting | bytes 8421376 | tf_op jit(solution)/shard_map/reshape | solution.py:97
  321.2 3.2 slice_reduce_fusion
  324.5 0.8 copy.31
  325.3 0.8 copy.32
  326.2 61.5 %psum.7 = f32[32,128]{1,0:T(8,128)S(1)} all-reduce(f32[32,128]{1,0:T(8,128)S(1)} %rev.7), channel_id=1, replica_groups=mesh['row'=16,'col'=16] {'row'}, use_global_device_ids=true, to_apply=%region_3.0 | all-reduce | flops 4096 | bytes 32768 | tf_op jit(solution)/shard_map/psum | solution.py:99
  387.7 0.6 broadcast_multiply_fusion
  388.3 7.7 %convolution_convert_fusion.2 = bf16[256,512]{1,0:T(8,128)(2,1)} fusion(bf16[256,8192]{0,1:T(8,128)(2,1)} %bitcast.61, bf16[8192,512]{1,0:T(8,128)(2,1)} %all-gather.2.cloned.1.call-done), kind=kOutput, calls=%fused_computation.9 | convolution fusion | flops 2147614720 | bytes 12845056 | tf_op jit(solution)/shard_map/dot_general | solution.py:72
  396.0 19.7 %reduce-scatter.5.cloned.1.call-done = bf16[512,512]{1,0:T(8,128)(2,1)} async-done(((bf16[8192,512]{1,0:T(8,128)(2,1)}), bf16[512,512]{1,0:T(8,128)(2,1)}) %reduce-scatter.5.cloned.1.call-update) | async-done | bytes 524304 | tf_op jit(solution)/shard_map/reduce_scatter | solution.py:100
  415.7 1.9 multiply_convert_fusion
  (46 shorter events, 1.3 us)
Async XLA Ops:
  7.2 83.1 %copy-start = (bf16[256,512]{1,0:T(8,128)(2,1)S(1)}, bf16[256,512]{1,0:T(8,128)(2,1)}, u32[]{:S(2)}) copy-start(bf16[256,512]{1,0:T(8,128)(2,1)} %param.11) | copy-start | bytes 786436
  7.2 83.1 %all-gather.2.cloned.1.call-start = ((), (), s32[]{:S(2)}) async-start(), calls=%async_computation.3 | async-start | bytes 8912896 | tf_op jit(solution)/shard_map/all_gather | solution.py:71
  7.9 170.9 %reduce-scatter.3.cloned.1.call-start = ((), (), s32[]{:S(2)}) async-start(), calls=%async_computation.4 | async-start | bytes 4456448 | tf_op jit(solution)/shard_map/reduce_scatter | solution.py:77
  98.0 0.9 copy-start.6
  98.0 3.3 copy-start.7
  98.0 5.7 %copy-start.8 = (f32[32,128]{1,0:T(8,128)S(1)}, f32[32,128]{1,0:T(8,128)}, u32[]{:S(2)}) copy-start(f32[32,128]{1,0:T(8,128)} %param.9) | copy-start | bytes 49156
  98.1 317.7 %reduce-scatter.5.cloned.1.call-start = ((), (), s32[]{:S(2)}) async-start(), calls=%async_computation.5 | async-start | bytes 8912896 | tf_op jit(solution)/shard_map/reduce_scatter | solution.py:100
  99.1 83.5 %collective-permute-start = (bf16[128,512]{0,1:T(8,128)(2,1)S(1)}, bf16[128,512]{0,1:T(8,128)(2,1)S(1)}, u32[]{:S(2)}, u32[]{:S(2)}) collective-permute-start(bf16[128,512]{0,1:T(8,128)(2,1)S(1)} %slice.34), channel_id=1, source_target_pairs={{0,16},{16,32},{32,48},{48,64},{64,80},{80,96},{96,112},{112,128},... | collective-permute-start | bytes 393224 | tf_op jit(solution)/shard_map/ppermute | solution.py:11
  101.5 81.2 %collective-permute-start.1 = (bf16[128,512]{0,1:T(8,128)(2,1)S(1)}, bf16[128,512]{0,1:T(8,128)(2,1)S(1)}, u32[]{:S(2)}, u32[]{:S(2)}) collective-permute-start(bf16[128,512]{0,1:T(8,128)(2,1)S(1)} %slice.35), channel_id=1, source_target_pairs={{0,16},{16,32},{32,48},{48,64},{64,80},{80,96},{96,112},{112,128},... | collective-permute-start | bytes 393224 | tf_op jit(solution)/shard_map/ppermute | solution.py:11
  113.6 2.2 slice-start
  129.1 2.2 slice-start.1
  131.3 47.5 %copy-start.2 = (bf16[256,512]{1,0:T(8,128)(2,1)S(1)}, bf16[256,512]{1,0:T(8,128)(2,1)}, u32[]{:S(2)}) copy-start(bf16[256,512]{1,0:T(8,128)(2,1)} %param.6) | copy-start | bytes 786436
  180.5 4.7 %collective-permute-start.2 = (bf16[128,512]{1,0:T(8,128)(2,1)}, bf16[128,512]{1,0:T(8,128)(2,1)S(1)}, u32[]{:S(2)}, u32[]{:S(2)}) collective-permute-start(bf16[128,512]{1,0:T(8,128)(2,1)} %slice.42), channel_id=1, source_target_pairs={{16,0},{32,16},{48,32},{64,48},{80,64},{96,80},{112,96},{128,112},... | collective-permute-start | bytes 393224 | tf_op jit(solution)/shard_map/ppermute | solution.py:11
  193.7 6.5 %copy-start.3 = (bf16[256,512]{1,0:T(8,128)(2,1)S(1)}, bf16[256,512]{1,0:T(8,128)(2,1)}, u32[]{:S(2)}) copy-start(bf16[256,512]{1,0:T(8,128)(2,1)} %reduce-scatter.3.cloned.1.call-done) | copy-start | bytes 786436
  297.1 2.1 copy-start.1
  313.0 11.5 %copy-start.5 = (bf16[256,512]{0,1:T(8,128)(2,1)S(1)}, bf16[256,512]{0,1:T(8,128)(2,1)}, u32[]{:S(2)}) copy-start(bf16[256,512]{0,1:T(8,128)(2,1)} %get-tuple-element.13) | copy-start | bytes 786436
  313.0 12.3 %copy-start.4 = (bf16[256,512]{0,1:T(8,128)(2,1)S(1)}, bf16[256,512]{0,1:T(8,128)(2,1)}, u32[]{:S(2)}) copy-start(bf16[256,512]{0,1:T(8,128)(2,1)} %get-tuple-element.12) | copy-start | bytes 786436
Sparse Core Ops, SparseCore 0:
  10.7 79.5 all-gather.1
  98.2 80.5 reduce-scatter.2
  304.9 110.8 reduce-scatter.4
